TPU v7x, 32 devices: a whole 2x2x4 slice. The times are simulated.
32 devices in a mesh: ep: 8 (over z, x), dp: 4 (over y, core).
Axes of the slice: x: 2, y: 2, z: 4, core: 2. Of those that a mesh axis runs over, the one named last changes fastest.
Arguments:
- residual: bfloat16 [4096, 2880], P(('ep', 'dp')), may hold values from -400 to 400, as said below
- norm_gain: float32 [2880], replicated, may hold values from 0.25 to 1.75
- router_weight: bfloat16 [2880, 32], replicated, may hold values from -0.109375 to 0.109375
- out_grad: bfloat16 [4096, 2880], P(('ep', 'dp')), may hold values from -6 to 6
- expert_ids: int32 [4096, 4], P(('ep', 'dp')), may hold values from 0 to 31, all different within a row; in each aligned block of 128 rows (0 to 127, 128 to 255, ...) at most 24 rows name the same one
- hidden: bfloat16 [32, 768, 1440], P(('ep', 'dp')), may hold values from -0.3125 to 0.3125
- down_weight: bfloat16 [32, 1440, 2880], P(('ep', 'dp')), may hold values from -0.15625 to 0.15625
Outputs:
- hidden_grad: bfloat16 [32, 768, 1440], P(('ep', 'dp'))
- down_weight_grad: bfloat16 [32, 1440, 2880], P(('ep', 'dp'))
- residual_grad: bfloat16 [4096, 2880], P(('ep', 'dp'))
- router_grad: float32 [2880, 32], replicated
- gain_grad: float32 [2880], replicated
Inputs may be any that keep to these rules, and one draw needn't show every extreme that they name: `expert_ids`: in the tokens of one device no expert is named more than 24 times, a bound that some block reaches. `residual`: Real-valued entries.
All inputs are finite; a program needn't handle non-finite values.
Results may differ from a plain program's by a relative error of at most 0.0085.
Values may be sent and summed in bfloat16 or wider, within the bound.
No kernel may reach another device: no remote copies, remote signals or barrier semaphores. Data moves between devices by JAX's collectives and lax.ppermute only.
A program may use at most 128 MiB of HBM per device.

v0:
```python
import jax
import jax.numpy as jnp
from jax import lax
from jax.sharding import PartitionSpec as P


def on_device(residual, norm_gain, router_weight, out_grad, expert_ids, hidden, down_weight):
    tokens_here, width = residual.shape
    top_count = expert_ids.shape[1]
    experts = router_weight.shape[1]
    slots = hidden.shape[1]
    capacity = slots // experts
    floated = residual.astype(jnp.float32)
    inverse = lax.rsqrt(jnp.mean(floated * floated, -1, keepdims=True) + 1e-05)
    unit = floated * inverse
    normed = (unit * norm_gain).astype(jnp.bfloat16)
    logits = jnp.dot(normed, router_weight, preferred_element_type=jnp.float32)
    match = expert_ids[:, :, None] == jnp.arange(experts, dtype=jnp.int32)[None, None, :]
    picked = jnp.sum(jnp.where(match, logits[:, None, :], jnp.float32(0.0)), -1)
    expo = jnp.exp(picked)
    prob = expo / jnp.sum(expo, -1, keepdims=True)
    flat_ids = expert_ids.reshape(-1)
    onehot = (flat_ids[:, None] == jnp.arange(experts, dtype=jnp.int32)[None, :]).astype(jnp.int32)
    slot_rank = jnp.sum((jnp.cumsum(onehot, 0) - onehot) * onehot, -1)
    place = flat_ids * capacity + slot_rank
    repeated = jnp.repeat(out_grad, top_count, axis=0)
    send_rows = jnp.zeros((experts * capacity, width), jnp.bfloat16).at[place].set(repeated)
    send_prob = (
        jnp.zeros((experts * capacity,), jnp.bfloat16)
        .at[place]
        .set(prob.astype(jnp.bfloat16).reshape(-1))
    )
    got_rows, got_prob = (
        lax.all_to_all(send_rows, ("ep", "dp"), split_axis=0, concat_axis=0, tiled=True),
        lax.all_to_all(send_prob, ("ep", "dp"), split_axis=0, concat_axis=0, tiled=True),
    )
    hidden_rows = hidden[0]
    weight = down_weight[0]
    inner = lax.dot_general(
        got_rows, weight, (((1,), (1,)), ((), ())), preferred_element_type=jnp.float32
    )
    slot_score = jnp.sum(inner * hidden_rows.astype(jnp.float32), -1)
    weight_col = got_prob.astype(jnp.float32)[:, None]
    hidden_grad = (weight_col * inner).astype(jnp.bfloat16)
    scaled = (weight_col * got_rows.astype(jnp.float32)).astype(jnp.bfloat16)
    weight_grad = lax.dot_general(
        hidden_rows, scaled, (((0,), (0,)), ((), ())), preferred_element_type=jnp.float32
    )
    came_back = lax.all_to_all(slot_score, ("ep", "dp"), split_axis=0, concat_axis=0, tiled=True)
    score = came_back[place].reshape(tokens_here, top_count)
    pick_grad = prob * (score - jnp.sum(prob * score, -1, keepdims=True))
    logit_grad = jnp.sum(jnp.where(match, pick_grad[:, :, None], jnp.float32(0.0)), 1)
    local_router = jnp.dot(
        normed.astype(jnp.float32).T, logit_grad, precision=lax.Precision.HIGHEST
    )
    normed_grad = jnp.dot(
        logit_grad, router_weight.astype(jnp.float32).T, precision=lax.Precision.HIGHEST
    )
    local_gain = jnp.sum(normed_grad * unit, 0)
    router_grad, gain_grad = lax.psum((local_router, local_gain), ("ep", "dp"))
    upper = normed_grad * norm_gain
    residual_grad = (inverse * (upper - unit * jnp.mean(upper * unit, -1, keepdims=True))).astype(
        jnp.bfloat16
    )
    return (
        hidden_grad[None],
        weight_grad.astype(jnp.bfloat16)[None],
        residual_grad,
        router_grad,
        gain_grad,
    )


def solution(mesh):
    return jax.shard_map(
        on_device,
        mesh=mesh,
        in_specs=(
            P(("ep", "dp"), None),
            P(),
            P(),
            P(("ep", "dp"), None),
            P(("ep", "dp"), None),
            P(("ep", "dp"), None, None),
            P(("ep", "dp"), None, None),
        ),
        out_specs=(
            P(("ep", "dp"), None, None),
            P(("ep", "dp"), None, None),
            P(("ep", "dp"), None),
            P(),
            P(),
        ),
        check_vma=False,
    )
```

profile of v0, /device:TPU:0, one launch (start us, length us, event | category | flops | bytes accessed | tf_op | source)
XLA Modules:
  0.0 325.0 jit_solution(3421626252912884726)
XLA Ops:
  7.2 0.0 copy-start
  7.2 0.0 copy-start.3
  7.2 0.0 copy-start.2
  7.2 0.8 broadcast_multiply_fusion
  8.0 0.8 copy.37
  8.8 0.1 eq.38
  8.9 0.1 eq.42
  9.0 0.1 copy.36
  9.1 0.1 mul.96
  9.2 1.2 reduce-window.6
  10.4 0.2 slice_reduce_fusion
  10.6 1.5 fusion.17
  12.2 0.0 copy-done
  12.2 1.7 fusion.20
  13.9 0.0 copy-done.3
  13.9 0.1 copy.40
  14.1 0.1 reshape.161
  14.2 0.1 fusion.24
  14.3 3.8 %scatter_custom_fusion = bf16[768]{0:T(1024)(128)(2,1)S(1)} fusion(s32[512]{0:T(512)S(1)} %bitcast.53, bf16[512]{0:T(512)(128)(2,1)S(1)} %reshape.161, bf16[]{:T(256)} %constant.7.clone.1), kind=kCustom, calls=%fused_computation.49 | custom fusion | bytes 1538 | tf_op jit(solution)/shard_map/scatter | solution.py:31
  18.1 0.7 all_to_all.30
  18.8 7.3 %all-to-all-start = ((bf16[32,24,1]{1,2,0:T(2,128)(2,1)}), bf16[32,24,1]{1,2,0:T(2,128)(2,1)S(1)}, u32[]{:S(2)}, u32[]{:S(2)}) async-start(bf16[32,24,1]{1,2,0:T(2,128)(2,1)} %all_to_all.30), calls=%async_computation | async-start | bytes 32768 | tf_op jit(solution)/shard_map/all_to_all | solution.py:35
  26.1 0.0 copy-done.2
  26.1 1.2 copy.44
  27.3 1.9 broadcast_in_dim.56
  29.2 2.9 reshape.169
  32.1 8.8 %scatter_custom_fusion.1 = bf16[768,2880]{1,0:T(8,128)(2,1)} fusion(s32[512]{0:T(512)S(1)} %bitcast.54, bf16[512,2880]{1,0:T(8,128)(2,1)} %reshape.169, bf16[]{:T(256)} %constant.7.clone.1), kind=kCustom, calls=%fused_computation.10 | custom fusion | bytes 4424192 | tf_op jit(solution)/shard_map/scatter | solution.py:27
  40.9 0.0 all-to-all-done
  40.9 5.9 %all-to-all-start.1 = ((bf16[32,24,2880]{2,1,0:T(8,128)(2,1)}), bf16[32,24,2880]{2,1,0:T(8,128)(2,1)}, u32[]{:S(2)}, u32[]{:S(2)}) async-start(bf16[32,24,2880]{2,1,0:T(8,128)(2,1)} %bitcast.51), calls=%async_computation.1 | async-start | bytes 9043968 | tf_op jit(solution)/shard_map/all_to_all | solution.py:34
  46.8 0.1 copy.42
  46.9 0.1 copy.43
  47.0 0.1 reshape.147
  47.1 0.1 copy.45
  47.2 100.9 %all-to-all-done.1 = bf16[32,24,2880]{2,1,0:T(8,128)(2,1)} async-done(((bf16[32,24,2880]{2,1,0:T(8,128)(2,1)}), bf16[32,24,2880]{2,1,0:T(8,128)(2,1)}, u32[]{:S(2)}, u32[]{:S(2)}) %all-to-all-start.1) | async-done | bytes 4423712 | tf_op jit(solution)/shard_map/all_to_all | solution.py:34
  148.1 12.2 %multiply_reduce_fusion = (f32[768]{0:T(1024)S(1)}, bf16[1,768,1440]{1,2,0:T(8,128)(2,1)}) fusion(bf16[1,768,1440]{1,2,0:T(8,128)(2,1)} %param.12, f32[768]{0:T(1024)S(1)} %reshape.147, bf16[768,2880]{1,0:T(8,128)(2,1)} %bitcast.4, bf16[1,1440,2880]{2,1,0:T(8,128)(2,1)} %param.13), kind=kOutput, calls=%fused_computation.8 | convolution fusion | flops 6375627776 | bytes 17147904 | tf_op jit(solution)/shard_map/dot_general | solution.py:39
  160.3 0.7 all_to_all.27
  161.0 5.2 %all-to-all-start.2 = ((f32[32,24,1]{1,2,0:T(1,128)}), f32[32,24,1]{1,2,0:T(1,128)S(1)}, u32[]{:S(2)}, u32[]{:S(2)}) async-start(f32[32,24,1]{1,2,0:T(1,128)} %bitcast.12), calls=%async_computation.2 | async-start | bytes 32768 | tf_op jit(solution)/shard_map/all_to_all | solution.py:49
  166.2 0.0 all-reduce.2.cloned.1.call-start
  166.3 0.0 copy-start.5
  166.3 3.8 %multiply_convert_fusion = bf16[32,24,2880]{2,1,0:T(8,128)(2,1)S(1)} fusion(bf16[32,24,2880]{2,1,0:T(8,128)(2,1)} %all-to-all-done.1, f32[32,24]{1,0:T(8,128)S(1)} %copy.45), kind=kLoop, calls=%fused_computation.5 | loop fusion | flops 6635520 | bytes 8850432 | tf_op jit(solution)/shard_map/convert_element_type | solution.py:45
  170.1 0.0 copy-done.5
  170.1 9.3 %fusion = bf16[1,1440,2880]{2,1,0:T(8,128)(2,1)} fusion(bf16[768,2880]{1,0:T(8,128)(2,1)S(1)} %bitcast.52, bf16[1,768,1440]{1,2,0:T(8,128)(2,1)S(1)} %copy-done.5), kind=kOutput, calls=%fused_computation.4 | convolution fusion | flops 6374246400 | bytes 14929920 | tf_op jit(solution)/shard_map/dot_general | solution.py:46
  179.4 0.0 copy-start.1
  179.4 0.0 copy-start.4
  179.4 0.0 all-to-all-done.2
  179.4 0.5 broadcast.113
  179.9 0.7 reduce.5
  180.6 0.1 all_to_all.29
  180.7 2.3 gather_fusion
  183.0 0.1 reshape.146
  183.1 0.1 copy.48
  183.3 0.0 copy-done.1
  183.3 0.0 copy-done.4
  183.3 1.7 fusion.16
  184.9 1.8 fusion.18
  186.7 0.0 all-reduce.2.cloned.1.call-update
  186.8 1.3 fusion.15
  188.1 40.6 %psum.15 = f32[2880]{0:T(1024)} all-reduce(f32[2880]{0:T(1024)S(1)} %get-tuple-element.5), channel_id=1, replica_groups=mesh['ep'=8,'dp'=4] {'ep','dp'}, use_global_device_ids=true, to_apply=%region_14.15 | all-reduce | flops 2880 | bytes 23040 | tf_op jit(solution)/shard_map/psum | solution.py:60
  228.7 87.7 %all-reduce.2.cloned.1.call-done = f32[2880,32]{0,1:T(8,128)} async-done(((f32[2880,32]{0,1:T(8,128)}), f32[2880,32]{0,1:T(8,128)}) %all-reduce.2.cloned.1.call-update) | async-done | bytes 368656 | tf_op jit(solution)/shard_map/psum | solution.py:60
  316.4 1.8 copy.52
  (14 shorter events, 0.2 us)
Async XLA Ops:
  7.2 5.0 %copy-start = (bf16[2880,32]{0,1:T(8,128)(2,1)S(1)}, bf16[2880,32]{0,1:T(8,128)(2,1)}, u32[]{:S(2)}) copy-start(bf16[2880,32]{0,1:T(8,128)(2,1)} %param.9) | copy-start | bytes 552964
  7.2 6.7 %copy-start.3 = (s32[128,4]{0,1:T(4,128)S(1)}, s32[128,4]{0,1:T(4,128)}, u32[]{:S(2)}) copy-start(s32[128,4]{0,1:T(4,128)} %param.11) | copy-start | bytes 6148
  7.2 18.9 %copy-start.2 = (bf16[128,2880]{0,1:T(8,128)(2,1)S(1)}, bf16[128,2880]{0,1:T(8,128)(2,1)}, u32[]{:S(2)}) copy-start(bf16[128,2880]{0,1:T(8,128)(2,1)} %param.10) | copy-start | bytes 2211844
  18.8 22.1 %all-to-all-start = ((bf16[32,24,1]{1,2,0:T(2,128)(2,1)}), bf16[32,24,1]{1,2,0:T(2,128)(2,1)S(1)}, u32[]{:S(2)}, u32[]{:S(2)}) async-start(bf16[32,24,1]{1,2,0:T(2,128)(2,1)} %all_to_all.30), calls=%async_computation | async-start | bytes 32768 | tf_op jit(solution)/shard_map/all_to_all | solution.py:35
  40.9 107.3 %all-to-all-start.1 = ((bf16[32,24,2880]{2,1,0:T(8,128)(2,1)}), bf16[32,24,2880]{2,1,0:T(8,128)(2,1)}, u32[]{:S(2)}, u32[]{:S(2)}) async-start(bf16[32,24,2880]{2,1,0:T(8,128)(2,1)} %bitcast.51), calls=%async_computation.1 | async-start | bytes 9043968 | tf_op jit(solution)/shard_map/all_to_all | solution.py:34
  161.0 18.4 %all-to-all-start.2 = ((f32[32,24,1]{1,2,0:T(1,128)}), f32[32,24,1]{1,2,0:T(1,128)S(1)}, u32[]{:S(2)}, u32[]{:S(2)}) async-start(f32[32,24,1]{1,2,0:T(1,128)} %bitcast.12), calls=%async_computation.2 | async-start | bytes 32768 | tf_op jit(solution)/shard_map/all_to_all | solution.py:49
  166.2 150.2 %all-reduce.2.cloned.1.call-start = ((), (), s32[]{:S(2)}) async-start(), calls=%async_computation.3 | async-start | bytes 753664 | tf_op jit(solution)/shard_map/psum | solution.py:60
  166.3 3.9 %copy-start.5 = (bf16[1,768,1440]{1,2,0:T(8,128)(2,1)S(1)}, bf16[1,768,1440]{1,2,0:T(8,128)(2,1)}, u32[]{:S(2)}) copy-start(bf16[1,768,1440]{1,2,0:T(8,128)(2,1)} %param.12) | copy-start | bytes 6635524
  179.4 3.8 %copy-start.1 = (bf16[128,2880]{0,1:T(8,128)(2,1)S(1)}, bf16[128,2880]{0,1:T(8,128)(2,1)}, u32[]{:S(2)}) copy-start(bf16[128,2880]{0,1:T(8,128)(2,1)} %param.7) | copy-start | bytes 2211844
  179.4 3.9 %copy-start.4 = (f32[2880]{0:T(1024)S(1)}, f32[2880]{0:T(1024)}, u32[]{:S(2)}) copy-start(f32[2880]{0:T(1024)} %param.8) | copy-start | bytes 34564
Sparse Core Ops, SparseCore 0:
  186.9 129.4 all-reduce.1
where the time goes:
time: 326 us; the launch traced here: 325 us
  waiting for transfers between devices  189 us (58%)
  blocking collectives  40.6 us (12%)
  local copies, waits for them, and re-layouts  26.7 us (8%)
  matrix products  26.6 us (8%)
  starting transfers between devices  18.5 us (6%)
  between operations  14.3 us (4%)
  other arithmetic  9.59 us (3%)
    all_to_all x1, waiting for transfers between devices, on_device(): lax.all_to_all(send_rows, ('ep', 'dp'), split_axis=0, concat_axis=0, tile...  101 us
    psum x1, waiting for transfers between devices, on_device(): router_grad, gain_grad = lax.psum((local_router, local_gain), ('ep', 'dp'))  87.7 us
    psum x1, blocking collectives, on_device(): router_grad, gain_grad = lax.psum((local_router, local_gain), ('ep', 'dp'))  40.6 us
    dot_general x1, matrix products, on_device(): lax.dot_general(got_rows, weight, (((1,), (1,)), ((), ())), preferred_ele...  12.2 us
    dot_general x1, matrix products, on_device(): lax.dot_general(hidden_rows, scaled, (((0,), (0,)), ((), ())), preferred_...  9.29 us
    scatter x1, local copies, waits for them, and re-layouts, on_device(): jnp.zeros((experts * capacity, width), jnp.bfloat16).at[place].set(repeated)  8.78 us
    all_to_all x1, starting transfers between devices, on_device(): lax.all_to_all(send_prob, ('ep', 'dp'), split_axis=0, concat_axis=0, tile...  7.33 us
  transfers between devices with their start and end apart: 4, of which 2 were waited for; matrix products, arithmetic and copies ran while one was open for 9% of the time, Pallas kernels for 0%

commit v1 on v0

v1 whole, which is shorter than its diff:
```python
import jax
import jax.numpy as jnp
from jax import lax
from jax.sharding import PartitionSpec as P

AXES = ("ep", "dp")


def on_device(residual, norm_gain, router_weight, out_grad, expert_ids, hidden, down_weight):
    tokens_here, width = residual.shape
    experts = router_weight.shape[1]
    slots = hidden.shape[1]
    capacity = slots // experts
    me = lax.axis_index(AXES)

    floated = residual.astype(jnp.float32)
    inverse = lax.rsqrt(jnp.mean(floated * floated, -1, keepdims=True) + 1e-05)
    unit = floated * inverse
    normed = (unit * norm_gain).astype(jnp.bfloat16)
    logits = jnp.dot(normed, router_weight, preferred_element_type=jnp.float32)
    names = jnp.arange(experts, dtype=jnp.int32)
    chosen = jnp.any(expert_ids[:, :, None] == names[None, None, :], 1)
    expo = jnp.where(chosen, jnp.exp(jnp.where(chosen, logits, 0.0)), 0.0)
    prob = expo / jnp.sum(expo, -1, keepdims=True)

    steps = jnp.arange(tokens_here, dtype=jnp.int32)
    earlier = (steps[:, None] > steps[None, :]).astype(jnp.bfloat16)
    rank = jnp.dot(earlier, chosen.astype(jnp.bfloat16), preferred_element_type=jnp.float32)
    owned = jnp.where(chosen, rank.astype(jnp.int32), -1).T
    select = owned[:, None, :] == jnp.arange(capacity, dtype=jnp.int32)[None, :, None]

    spare = -(width + experts) % 128
    packed = jnp.concatenate(
        [
            out_grad,
            prob.astype(jnp.bfloat16),
            jnp.zeros((tokens_here, spare), jnp.bfloat16),
        ],
        1,
    )
    onehot = select.astype(jnp.bfloat16).reshape(experts * capacity, tokens_here)
    send = jnp.dot(onehot, packed, preferred_element_type=jnp.float32).astype(jnp.bfloat16)
    got = lax.all_to_all(
        send.reshape(experts, capacity, -1), AXES, split_axis=0, concat_axis=0, tiled=True
    ).reshape(slots, -1)

    got_rows = got[:, :width]
    mine = jnp.arange(experts, dtype=jnp.int32)[None, :] == me
    tail = got[:, width : width + experts].astype(jnp.float32)
    weight_col = jnp.sum(jnp.where(mine, tail, 0.0), 1, keepdims=True)
    hidden_rows = hidden[0]
    weight = down_weight[0]
    inner = lax.dot_general(
        got_rows, weight, (((1,), (1,)), ((), ())), preferred_element_type=jnp.float32
    )
    slot_score = jnp.sum(inner * hidden_rows.astype(jnp.float32), -1)
    hidden_grad = (weight_col * inner).astype(jnp.bfloat16)
    scaled = (weight_col * got_rows.astype(jnp.float32)).astype(jnp.bfloat16)
    weight_grad = lax.dot_general(
        hidden_rows, scaled, (((0,), (0,)), ((), ())), preferred_element_type=jnp.float32
    )

    came_back = lax.all_to_all(
        slot_score.reshape(experts, capacity), AXES, split_axis=0, concat_axis=0, tiled=True
    )
    score = jnp.sum(jnp.where(select, came_back[:, :, None], 0.0), 1).T
    logit_grad = prob * (score - jnp.sum(prob * score, -1, keepdims=True))

    local_router = lax.dot_general(
        logit_grad,
        normed.astype(jnp.float32),
        (((0,), (0,)), ((), ())),
        precision=lax.Precision.HIGHEST,
    )
    pieces = lax.all_to_all(local_router, AXES, split_axis=0, concat_axis=0, tiled=True)
    total = jnp.sum(pieces, 0, keepdims=True)
    router_rows = lax.all_to_all(
        jnp.broadcast_to(total, (experts, width)), AXES, split_axis=0, concat_axis=0, tiled=True
    )
    gain_grad = jnp.sum(router_rows * router_weight.T.astype(jnp.float32), 0) / norm_gain

    normed_grad = jnp.dot(
        logit_grad, router_weight.astype(jnp.float32).T, precision=lax.Precision.HIGHEST
    )
    upper = normed_grad * norm_gain
    residual_grad = (inverse * (upper - unit * jnp.mean(upper * unit, -1, keepdims=True))).astype(
        jnp.bfloat16
    )
    return (
        hidden_grad[None],
        weight_grad.astype(jnp.bfloat16)[None],
        residual_grad,
        router_rows.T,
        gain_grad,
    )


def solution(mesh):
    return jax.shard_map(
        on_device,
        mesh=mesh,
        in_specs=(
            P(AXES, None),
            P(),
            P(),
            P(AXES, None),
            P(AXES, None),
            P(AXES, None, None),
            P(AXES, None, None),
        ),
        out_specs=(
            P(AXES, None, None),
            P(AXES, None, None),
            P(AXES, None),
            P(),
            P(),
        ),
        check_vma=False,
    )
```

time: 326 us -> 183 us (0.56)
  waiting for transfers between devices: 189 us -> 113 us
  blocking collectives: 40.6 us -> 12.2 us
  local copies, waits for them, and re-layouts: 26.7 us -> 3.1 us
  between operations: 14.3 us -> 0.8 us
  matrix products: 26.6 us -> 31.6 us
  other arithmetic: 9.59 us -> 5.89 us
    psum x1 -> x0, waiting for transfers between devices: 87.7 us -> none  [on_device(): router_grad, gain_grad = lax.psum((local_router, local_gain), ('ep', 'dp'))]
    psum x1 -> x0, blocking collectives: 40.6 us -> none  [on_device(): router_grad, gain_grad = lax.psum((local_router, local_gain), ('ep', 'dp'))]
    scatter x2 -> x0, local copies, waits for them, and re-layouts: 12.5 us -> none  [the longest x1 8.78 us: on_device(): jnp.zeros((experts * capacity, width), jnp.bfloat16).at[place].set(repeated)]
    all_to_all x0 -> x1, blocking collectives: none -> 12.2 us  [on_device(): lax.all_to_all(slot_score.reshape(experts, capacity), AXES, split_axis=0,...]
    all_to_all x3, waiting for transfers between devices: 101 us -> 113 us  [the longest x1 101 us: on_device(): lax.all_to_all(send.reshape(experts, capacity, -1), AXES, split_axis=0, c...]
    convert_element_type x4 -> x1, other arithmetic: 3.86 us -> 0.01 us  [on_device(): prob.astype(jnp.bfloat16)]
  transfers between devices with their start and end apart: 4 -> 3, of which waited for: 2 -> 2; matrix products, arithmetic and copies ran while one was open for 9% -> 8% of each run, Pallas kernels for 0% -> 0%
where the time goes in v1:
time: 183 us
  waiting for transfers between devices  113 us (62%)
  matrix products  31.6 us (17%)
  starting transfers between devices  15.9 us (9%)
  blocking collectives  12.2 us (7%)
  other arithmetic  5.89 us (3%)
  local copies, waits for them, and re-layouts  3.1 us (2%)
    all_to_all x1, waiting for transfers between devices, on_device(): lax.all_to_all(send.reshape(experts, capacity, -1), AXES, split_axis=0, c...  101 us
    all_to_all x1, blocking collectives, on_device(): lax.all_to_all(slot_score.reshape(experts, capacity), AXES, split_axis=0,...  12.2 us
    dot_general x1, matrix products, on_device(): lax.dot_general(hidden_rows, scaled, (((0,), (0,)), ((), ())), preferred_...  12.1 us
    dot_general x1, matrix products, on_device(): lax.dot_general(got_rows, weight, (((1,), (1,)), ((), ())), preferred_ele...  11.9 us
    all_to_all x1, waiting for transfers between devices, on_device(): lax.all_to_all(jnp.broadcast_to(total, (experts, width)), AXES, split_axi...  11.8 us
    all_to_all x1, starting transfers between devices, on_device(): lax.all_to_all(send.reshape(experts, capacity, -1), AXES, split_axis=0, c...  7.44 us
    all_to_all x1, starting transfers between devices, on_device(): lax.all_to_all(jnp.broadcast_to(total, (experts, width)), AXES, split_axi...  5.83 us
  transfers between devices with their start and end apart: 3, of which 2 were waited for; matrix products, arithmetic and copies ran while one was open for 8% of the time, Pallas kernels for 0%

profile of v1, /device:TPU:0, one launch (start us, length us, event | category | flops | bytes accessed | tf_op | source)
XLA Modules:
  0.0 182.5 jit_solution(16902184673423157135)
XLA Ops:
  0.6 0.0 copy-start.2
  0.7 0.1 eq.56
  0.7 0.8 fusion.28
  1.5 0.1 fusion.19
  1.6 1.5 fusion.16
  3.2 0.2 bitcast_compare_fusion
  3.4 1.7 fusion.35
  5.1 0.1 pad.2.clone
  5.2 0.0 copy-done.2
  5.2 3.5 %convolution_convert_fusion.1 = bf16[768,2944]{1,0:T(8,128)(2,1)} fusion(pred[768,128]{1,0:T(32,128)(4,1)S(1)} %bitcast_compare_fusion, bf16[128,32]{0,1:T(8,128)(2,1)S(1)} %fusion.34, bf16[128,2880]{0,1:T(8,128)(2,1)S(1)} %copy-done.2, bf16[2944]{0:T(1024)(128)(2,1)S(1)} %pad.2.clone), kind=kOutput, calls=%fused_computation.5 | convolution fusion | flops 583335936 | bytes 5371648 | tf_op jit(solution)/shard_map/dot_general | solution.py:42
  8.7 0.0 copy-start.4
  8.7 7.4 %all-to-all-start = ((bf16[32,24,2944]{2,1,0:T(8,128)(2,1)}), bf16[32,24,2944]{2,1,0:T(8,128)(2,1)}, u32[]{:S(2)}, u32[]{:S(2)}) async-start(bf16[32,24,2944]{2,1,0:T(8,128)(2,1)} %bitcast.50), calls=%async_computation | async-start | bytes 9043968 | tf_op jit(solution)/shard_map/all_to_all | solution.py:43
  16.2 101.3 %all-to-all-done = bf16[32,24,2944]{2,1,0:T(8,128)(2,1)} async-done(((bf16[32,24,2944]{2,1,0:T(8,128)(2,1)}), bf16[32,24,2944]{2,1,0:T(8,128)(2,1)}, u32[]{:S(2)}, u32[]{:S(2)}) %all-to-all-start) | async-done | bytes 4522016 | tf_op jit(solution)/shard_map/all_to_all | solution.py:43
  117.5 1.1 select_reduce_fusion.1
  118.6 0.0 copy-done.4
  118.6 0.0 copy-start
  118.7 0.0 copy-start.3
  118.7 11.9 %multiply_reduce_fusion = (f32[768]{0:T(1024)S(1)}, bf16[1,768,1440]{1,2,0:T(8,128)(2,1)}) fusion(bf16[1,768,1440]{1,2,0:T(8,128)(2,1)S(1)} %copy-done.4, f32[768]{0:T(1024)S(1)} %select_reduce_fusion.1, bf16[1,1440,2880]{2,1,0:T(8,128)(2,1)} %param.13, bf16[768,2944]{1,0:T(8,128)(2,1)} %bitcast.3), kind=kOutput, calls=%fused_computation.7 | convolution fusion | flops 6375627776 | bytes 17246208 | tf_op jit(solution)/shard_map/dot_general | solution.py:53
  130.6 0.1 all_to_all.22
  130.7 12.2 %all_to_all.32 = f32[32,1,24]{2,1,0:T(1,128)S(1)} all-to-all(f32[32,1,24]{2,1,0:T(1,128)S(1)} %bitcast.53), channel_id=1, replica_groups=mesh['ep'=8,'dp'=4] {'ep','dp'}, dimensions={0} | all-to-all | bytes 6144 | tf_op jit(solution)/shard_map/all_to_all | solution.py:63
  142.9 0.2 select_reduce_fusion
  143.1 0.0 copy-done
  143.1 0.0 copy-done.3
  143.1 1.0 convolution_bitcast_fusion
  144.1 1.1 copy.18
  145.3 2.6 %all-to-all-start.2 = ((f32[32,1,2880]{2,1,0:T(1,128)}), f32[32,1,2880]{2,1,0:T(1,128)S(1)}, u32[]{:S(2)}, u32[]{:S(2)}) async-start(f32[32,1,2880]{2,1,0:T(1,128)} %copy.18), calls=%async_computation.2 | async-start | bytes 753664 | tf_op jit(solution)/shard_map/all_to_all | solution.py:75
  147.9 0.0 copy-start.1
  147.9 12.1 %fusion = bf16[1,1440,2880]{2,1,0:T(8,128)(2,1)} fusion(f32[768]{0:T(1024)S(1)} %select_reduce_fusion.1, bf16[768,2944]{1,0:T(8,128)(2,1)} %bitcast.3, bf16[1,768,1440]{1,2,0:T(8,128)(2,1)} %param.12), kind=kOutput, calls=%fused_computation.1 | convolution fusion | flops 6380881920 | bytes 15031296 | tf_op jit(solution)/shard_map/dot_general | solution.py:59
  160.0 0.0 copy-done.1
  160.0 1.1 fusion.12
  161.1 0.0 all-to-all-done.2
  161.1 0.2 reduce_sum.88
  161.4 0.9 broadcast_in_dim.75
  162.3 5.8 %all-to-all-start.3 = ((f32[32,1,2880]{2,1,0:T(1,128)}), f32[32,1,2880]{2,1,0:T(1,128)S(1)}, u32[]{:S(2)}, u32[]{:S(2)}) async-start(f32[32,1,2880]{2,1,0:T(1,128)} %broadcast_in_dim.75), calls=%async_computation.3 | async-start | bytes 753664 | tf_op jit(solution)/shard_map/all_to_all | solution.py:77
  168.1 1.2 fusion.15
  169.3 11.8 %all-to-all-done.3 = f32[32,1,2880]{2,1,0:T(1,128)S(1)} async-done(((f32[32,1,2880]{2,1,0:T(1,128)}), f32[32,1,2880]{2,1,0:T(1,128)S(1)}, u32[]{:S(2)}, u32[]{:S(2)}) %all-to-all-start.3) | async-done | bytes 368672 | tf_op jit(solution)/shard_map/all_to_all | solution.py:77
  181.1 0.1 fusion.25
  181.2 0.6 div.21
  181.8 0.8 copy.22
  (7 shorter events, 0.1 us)
Async XLA Ops:
  0.6 4.6 %copy-start.2 = (bf16[128,2880]{0,1:T(8,128)(2,1)S(1)}, bf16[128,2880]{0,1:T(8,128)(2,1)}, u32[]{:S(2)}) copy-start(bf16[128,2880]{0,1:T(8,128)(2,1)} %param.10) | copy-start | bytes 2211844
  8.7 109.9 %copy-start.4 = (bf16[1,768,1440]{1,2,0:T(8,128)(2,1)S(1)}, bf16[1,768,1440]{1,2,0:T(8,128)(2,1)}, u32[]{:S(2)}) copy-start(bf16[1,768,1440]{1,2,0:T(8,128)(2,1)} %param.12) | copy-start | bytes 6635524
  8.7 108.8 %all-to-all-start = ((bf16[32,24,2944]{2,1,0:T(8,128)(2,1)}), bf16[32,24,2944]{2,1,0:T(8,128)(2,1)}, u32[]{:S(2)}, u32[]{:S(2)}) async-start(bf16[32,24,2944]{2,1,0:T(8,128)(2,1)} %bitcast.50), calls=%async_computation | async-start | bytes 9043968 | tf_op jit(solution)/shard_map/all_to_all | solution.py:43
  118.6 24.4 %copy-start = (bf16[128,2880]{0,1:T(8,128)(2,1)S(1)}, bf16[128,2880]{0,1:T(8,128)(2,1)}, u32[]{:S(2)}) copy-start(bf16[128,2880]{0,1:T(8,128)(2,1)} %param.7) | copy-start | bytes 2211844
  118.7 24.4 %copy-start.3 = (f32[2880]{0:T(1024)S(1)}, f32[2880]{0:T(1024)}, u32[]{:S(2)}) copy-start(f32[2880]{0:T(1024)} %param.8) | copy-start | bytes 34564
  145.3 15.9 %all-to-all-start.2 = ((f32[32,1,2880]{2,1,0:T(1,128)}), f32[32,1,2880]{2,1,0:T(1,128)S(1)}, u32[]{:S(2)}, u32[]{:S(2)}) async-start(f32[32,1,2880]{2,1,0:T(1,128)} %copy.18), calls=%async_computation.2 | async-start | bytes 753664 | tf_op jit(solution)/shard_map/all_to_all | solution.py:75
  147.9 12.1 %copy-start.1 = (bf16[2880,32]{0,1:T(8,128)(2,1)S(1)}, bf16[2880,32]{0,1:T(8,128)(2,1)}, u32[]{:S(2)}) copy-start(bf16[2880,32]{0,1:T(8,128)(2,1)} %param.9) | copy-start | bytes 552964
  162.3 18.8 %all-to-all-start.3 = ((f32[32,1,2880]{2,1,0:T(1,128)}), f32[32,1,2880]{2,1,0:T(1,128)S(1)}, u32[]{:S(2)}, u32[]{:S(2)}) async-start(f32[32,1,2880]{2,1,0:T(1,128)} %broadcast_in_dim.75), calls=%async_computation.3 | async-start | bytes 753664 | tf_op jit(solution)/shard_map/all_to_all | solution.py:77
